TPU v7x, 32 devices: a whole 2x2x4 slice. The times are simulated.
32 devices in a mesh: pb: 4 (over z), row: 4 (over y, x), col: 2 (over core).
Axes of the slice: x: 2, y: 2, z: 4, core: 2. Of those that a mesh axis runs over, the one named last changes fastest.
Arguments:
- amplitudes: bfloat16 [4, 20, 4, 9216], P('pb'), may hold values from -6 to 6
- pairs: int32 [4, 4, 2], P('pb'), may hold values from 0 to 3
- stored_k: int32 [4], replicated, may hold values from 0 to 3, each once
- orbitals: bfloat16 [4, 192, 2048], P('pb', None, ('row', 'col')), may hold values from -1.078125 to 1.078125
- valence_energy: float32 [4, 96], replicated, may hold values from -1 to 0
- conduction_energy: float32 [4, 96], replicated, may hold values from 2.5 to 3.5
- screened: bfloat16 [4, 2048, 2048], P('pb', 'row', 'col'), may hold values from -0.125 to 0.125
Outputs:
- filtered: bfloat16 [4, 20, 4, 9216], P('pb')
Inputs may be any that keep to these rules, and one draw needn't show every extreme that they name: stored_k holds every k-point exactly once; row s of orbitals belongs to k-point stored_k[s]. `pairs`: each entry is a k-point.
All inputs are finite; a program needn't handle non-finite values.
Results may differ from a plain program's by a relative error of at most 0.024.
Values may be sent and summed in bfloat16 or wider, within the bound.
A program may use at most 64 MiB of HBM per device.

v0:
```python
import jax
import jax.numpy as jnp
from jax import lax
from jax.sharding import PartitionSpec as P

CENTER = 3.0
HALF = 2.5


def on_device(amplitudes, pairs, stored_k, orbitals, valence_energy, conduction_energy, screened):
    amplitude = amplitudes[0]
    pair_list = pairs[0]
    w_tile = screened[0]
    count_v = valence_energy.shape[1]
    count_c = conduction_energy.shape[1]
    vectors, pair_count, flat_size = amplitude.shape
    points = orbitals.shape[2]
    col_width = w_tile.shape[1]
    column = lax.axis_index("col")

    def pick(shard_piece):
        pick_low = (stored_k[None, :] == pair_list[:, 0:1]).astype(jnp.bfloat16)
        pick_high = (stored_k[None, :] == pair_list[:, 1:2]).astype(jnp.bfloat16)
        low_bands = jnp.einsum(
            "pl,lbr->pbr", pick_low, shard_piece[:, :count_v], preferred_element_type=jnp.float32
        )
        high_bands = jnp.einsum(
            "pl,lbr->pbr", pick_high, shard_piece[:, count_v:], preferred_element_type=jnp.float32
        )
        return (low_bands, high_bands)

    def fetch_each():
        found = pick(lax.all_gather(orbitals, "pb", axis=0, tiled=True))
        return (found[0].astype(jnp.bfloat16), found[1].astype(jnp.bfloat16))

    low_energy = jnp.take(valence_energy, pair_list[:, 0], axis=0)
    high_energy = jnp.take(conduction_energy, pair_list[:, 1], axis=0)
    gap_grid = (high_energy[:, None, :] - low_energy[:, :, None]).reshape(pair_count, flat_size)
    gap_rows = jnp.tile(gap_grid, (vectors, 1))

    def kernel_term(current, bands):
        valence, conduction_orbital = bands
        amplitude_lattice = current.reshape(vectors, pair_count, count_v, count_c)
        inner_total_sum = jnp.einsum(
            "iomx,oxj->iomj",
            amplitude_lattice,
            conduction_orbital,
            preferred_element_type=jnp.float32,
        )
        values = jnp.sum(valence.astype(jnp.float32)[None] * inner_total_sum, axis=2)
        values = values.astype(jnp.bfloat16).reshape(vectors * pair_count, points)
        everywhere = lax.all_gather(values, ("row", "col"), axis=1, tiled=True)
        needed = lax.dynamic_slice_in_dim(everywhere, column * col_width, col_width, 1)
        partial_value = lax.dot_general(
            needed, w_tile, (((1,), (1,)), ((), ())), preferred_element_type=jnp.float32
        )
        own_sums = (
            lax.psum_scatter(
                partial_value.astype(jnp.bfloat16), "col", scatter_dimension=1, tiled=True
            )
            .astype(jnp.float32)
            .reshape(vectors, pair_count, points)
        )
        weighted_product = (valence.astype(jnp.float32)[None] * own_sums[:, :, None, :]).astype(
            jnp.bfloat16
        )
        projected = jnp.einsum(
            "kyqz,yhz->kyqh",
            weighted_product,
            conduction_orbital,
            preferred_element_type=jnp.float32,
        )
        return projected.reshape(vectors * pair_count, flat_size)

    def advance(current_rows, summed, gap_part, previous_rows, factor):
        value = (gap_part * current_rows + summed - CENTER * current_rows) / HALF
        if previous_rows is None:
            return value.astype(jnp.bfloat16)
        return (factor * value - previous_rows).astype(jnp.bfloat16)

    def finish(partial_term, current, previous, factor):
        summed = lax.psum(partial_term.astype(jnp.bfloat16), ("row", "col")).astype(jnp.float32)
        previous_full = None
        if previous is not None:
            previous_full = previous.astype(jnp.float32)
        return advance(current.astype(jnp.float32), summed, gap_rows, previous_full, factor)

    initial = amplitude.reshape(vectors * pair_count, flat_size)
    first_bands = fetch_each()
    first_term = finish(kernel_term(initial, first_bands), initial, None, 1.0)
    second_bands = fetch_each()
    second_term = finish(kernel_term(first_term, second_bands), first_term, initial, 2.0)
    return second_term.reshape(1, vectors, pair_count, flat_size)


def solution(mesh):
    return jax.shard_map(
        on_device,
        mesh=mesh,
        in_specs=(
            P("pb", None, None, None),
            P("pb", None, None),
            P(),
            P("pb", None, ("row", "col")),
            P(),
            P(),
            P("pb", "row", "col"),
        ),
        out_specs=P("pb", None, None, None),
        check_vma=False,
    )
```

profile of v0, /device:TPU:0, one launch (start us, length us, event | category | flops | bytes accessed | tf_op | source)
XLA Modules:
  0.0 231.6 jit_solution(977043757335007725)
XLA Ops:
  6.5 0.0 copy-start
  6.5 0.0 copy-start.1
  6.5 0.0 reduce-scatter.3.cloned.1.call-start
  6.5 0.8 slice_bitcast_fusion.1
  7.4 0.0 copy-start.5
  7.4 16.6 %all_gather.10 = bf16[4,192,256]{2,1,0:T(8,128)(2,1)S(1)} all-gather(bf16[1,192,256]{2,1,0:T(8,128)(2,1)} %param.12), channel_id=1, replica_groups=mesh['pb'=4,'row'=4,'col'=2] {'pb'}, dimensions={0}, use_global_device_ids=true | all-gather | bytes 491520 | tf_op jit(solution)/shard_map/all_gather | solution.py:33
  24.0 1.0 fusion.15
  25.0 0.1 copy.59
  25.1 0.0 copy-done.1
  25.1 2.6 %reshape_reshape_squeeze.3 = bf16[20,4,96,96]{3,2,1,0:T(8,128)(2,1)} reshape(bf16[1,20,4,9216]{3,2,1,0:T(4,128)(2,1)S(1)} %copy-done.1) | data formatting | bytes 2949120 | tf_op jit(solution)/shard_map/reshape;reshape;squeeze | solution.py:43
  27.7 0.0 copy-done.5
  27.7 0.3 fusion.16
  28.0 0.0 copy-start.6
  28.0 2.8 %fusion.1 = bf16[20,4,256]{2,0,1:T(8,128)(2,1)S(1)} fusion(f32[4,96,256]{2,1,0:T(8,128)S(1)} %copy.59, bf16[20,4,96,96]{3,2,1,0:T(8,128)(2,1)} %reshape_reshape_squeeze.3, bf16[4,96,256,1]{2,0,1,3:T(4,128)(2,1)S(1)} %fusion.16), kind=kOutput, calls=%fused_computation.5 | convolution fusion | flops 381399040 | bytes 2105344 | tf_op jit(solution)/shard_map/iomx,oxj->iomj/dot_general | solution.py:44
  30.8 0.0 copy-done.6
  30.9 10.1 %all_gather.11 = bf16[80,2048]{1,0:T(8,128)(2,1)S(1)} all-gather(bf16[80,256]{1,0:T(8,128)(2,1)S(1)} %convert_element_type.92), channel_id=1, replica_groups=mesh['pb'=4,'row'=4,'col'=2] {'row','col'}, dimensions={1}, use_global_device_ids=true | all-gather | bytes 368640 | tf_op jit(solution)/shard_map/all_gather | solution.py:52
  41.0 0.0 copy-start.4
  41.0 0.0 copy-done
  41.0 1.1 convolution_convert_fusion.3
  42.1 0.0 copy-start.7
  42.1 0.0 reduce-scatter.3.cloned.1.call-update
  42.1 0.0 all-reduce.3.cloned.1.call-start
  42.2 1.7 reshape.48
  43.9 0.0 copy-done.4
  43.9 6.7 %reduce-scatter.3.cloned.1.call-done = bf16[80,256]{1,0:T(8,128)(2,1)} async-done(((bf16[80,512]{1,0:T(8,128)(2,1)}), bf16[80,256]{1,0:T(8,128)(2,1)}) %reduce-scatter.3.cloned.1.call-update) | async-done | bytes 40976 | tf_op jit(solution)/shard_map/reduce_scatter | solution.py:58
  50.6 0.8 reshape.49
  51.4 0.0 copy-done.7
  51.4 2.9 %convert_bitcast_fusion.1 = bf16[20,4,96,96]{2,3,0,1:T(8,128)(2,1)} fusion(f32[20,4,256]{2,0,1:T(8,128)S(1)} %copy.63, f32[4,96,256]{2,1,0:T(8,128)S(1)} %copy.59, bf16[4,96,256,1]{2,0,1,3:T(4,128)(2,1)S(1)} %copy-done.7), kind=kOutput, calls=%fused_computation.25 | convolution fusion | flops 382156800 | bytes 2146304 | tf_op jit(solution)/shard_map/kyqz,yhz->kyqh/dot_general | solution.py:67
  54.3 3.2 %copy.65 = bf16[20,4,96,96]{3,2,1,0:T(8,128)(2,1)S(1)} copy(bf16[20,4,96,96]{2,3,0,1:T(8,128)(2,1)} %convert_bitcast_fusion.1) | data formatting | bytes 2949120 | tf_op jit(solution)/shard_map/convert_element_type | solution.py:82
  57.5 0.0 copy-start.2
  57.5 0.0 copy-start.3
  57.6 3.6 %convert_element_type.97 = bf16[80,9216]{1,0:T(8,128)(2,1)} reshape(bf16[20,4,96,96]{3,2,1,0:T(8,128)(2,1)S(1)} %copy.65) | data formatting | bytes 2949120 | tf_op jit(solution)/shard_map/convert_element_type | solution.py:82
  61.1 0.0 all-reduce.3.cloned.1.call-update
  61.1 0.0 reduce-scatter.5.cloned.1.call-start
  61.2 0.0 copy-done.2
  61.2 0.6 gather_fusion.1
  61.8 0.0 copy-done.3
  61.8 0.6 gather_fusion
  62.3 0.1 broadcast_select_fusion
  62.4 0.1 broadcast_select_fusion.1
  62.5 0.1 broadcast_subtract_fusion
  62.6 0.2 sub.32
  62.8 2.3 tile.8
  65.0 4.3 %tile.9 = f32[80,9216]{1,0:T(8,128)} reshape(f32[20,4,9216]{2,1,0:T(4,128)} %tile.8) | data formatting | bytes 5898240 | tf_op jit(solution)/shard_map/tile | solution.py:39
  69.3 51.5 %all-reduce.3.cloned.1.call-done = bf16[80,9216]{1,0:T(8,128)(2,1)} async-done(((bf16[80,9216]{1,0:T(8,128)(2,1)}), bf16[80,9216]{1,0:T(8,128)(2,1)}) %all-reduce.3.cloned.1.call-update) | async-done | bytes 1474576 | tf_op jit(solution)/shard_map/psum | solution.py:82
  120.8 3.8 %multiply_convert_fusion.4 = bf16[80,9216]{1,0:T(8,128)(2,1)S(1)} fusion(f32[80,9216]{1,0:T(8,128)} %reshape.48, bf16[80,9216]{1,0:T(8,128)(2,1)} %all-reduce.3.cloned.1.call-done, f32[80,9216]{1,0:T(8,128)} %tile.9), kind=kLoop, calls=%fused_computation.21 | loop fusion | flops 5160960 | bytes 8847360 | tf_op jit(solution)/shard_map/convert_element_type | solution.py:78
  124.6 0.0 copy-start.8
  124.6 2.9 %reshape.46 = bf16[20,4,96,96]{3,2,1,0:T(8,128)(2,1)} reshape(bf16[80,9216]{1,0:T(8,128)(2,1)S(1)} %multiply_convert_fusion.4) | data formatting | bytes 2949120 | tf_op jit(solution)/shard_map/reshape | solution.py:43
  127.6 0.0 copy-done.8
  127.6 2.7 %fusion = bf16[20,4,256]{2,0,1:T(8,128)(2,1)S(1)} fusion(f32[4,96,256]{2,1,0:T(8,128)S(1)} %copy.59, bf16[20,4,96,96]{3,2,1,0:T(8,128)(2,1)} %reshape.46, bf16[4,96,256,1]{2,0,1,3:T(4,128)(2,1)S(1)} %copy-done.8), kind=kOutput, calls=%fused_computation.3 | convolution fusion | flops 381399040 | bytes 2105344 | tf_op jit(solution)/shard_map/iomx,oxj->iomj/dot_general | solution.py:44
  130.4 9.5 %all_gather.12 = bf16[80,2048]{1,0:T(8,128)(2,1)S(1)} all-gather(bf16[80,256]{1,0:T(8,128)(2,1)S(1)} %convert_element_type.102), channel_id=1, replica_groups=mesh['pb'=4,'row'=4,'col'=2] {'row','col'}, dimensions={1}, use_global_device_ids=true | all-gather | bytes 368640 | tf_op jit(solution)/shard_map/all_gather | solution.py:52
  139.8 1.1 convolution_convert_fusion.2
  140.9 0.0 reduce-scatter.5.cloned.1.call-update
  140.9 0.2 all-reduce.5.cloned.1.call-start
  141.2 7.4 %reduce-scatter.5.cloned.1.call-done = bf16[80,256]{1,0:T(8,128)(2,1)} async-done(((bf16[80,512]{1,0:T(8,128)(2,1)}), bf16[80,256]{1,0:T(8,128)(2,1)}) %reduce-scatter.5.cloned.1.call-update) | async-done | bytes 40976 | tf_op jit(solution)/shard_map/reduce_scatter | solution.py:58
  148.6 0.8 reshape.50
  149.4 2.9 %convert_bitcast_fusion = bf16[20,4,96,96]{2,3,0,1:T(8,128)(2,1)} fusion(f32[20,4,256]{2,0,1:T(8,128)S(1)} %copy.69, f32[4,96,256]{2,1,0:T(8,128)S(1)} %copy.59, bf16[4,96,256,1]{2,0,1,3:T(4,128)(2,1)S(1)} %copy-done.8), kind=kOutput, calls=%fused_computation.24 | convolution fusion | flops 382156800 | bytes 2146304 | tf_op jit(solution)/shard_map/kyqz,yhz->kyqh/dot_general | solution.py:67
  152.3 3.2 %copy.71 = bf16[20,4,96,96]{3,2,1,0:T(8,128)(2,1)S(1)} copy(bf16[20,4,96,96]{2,3,0,1:T(8,128)(2,1)} %convert_bitcast_fusion) | data formatting | bytes 2949120 | tf_op jit(solution)/shard_map/convert_element_type | solution.py:82
  155.5 3.6 %convert_element_type.107 = bf16[80,9216]{1,0:T(8,128)(2,1)} reshape(bf16[20,4,96,96]{3,2,1,0:T(8,128)(2,1)S(1)} %copy.71) | data formatting | bytes 2949120 | tf_op jit(solution)/shard_map/convert_element_type | solution.py:82
  159.1 0.0 all-reduce.5.cloned.1.call-update
  159.1 59.7 %all-reduce.5.cloned.1.call-done = bf16[80,9216]{1,0:T(8,128)(2,1)} async-done(((bf16[80,9216]{1,0:T(8,128)(2,1)}), bf16[80,9216]{1,0:T(8,128)(2,1)}) %all-reduce.5.cloned.1.call-update) | async-done | bytes 1474576 | tf_op jit(solution)/shard_map/psum | solution.py:82
  218.8 4.8 %fusion.12 = bf16[80,9216]{1,0:T(8,128)(2,1)S(1)} fusion(f32[80,9216]{1,0:T(8,128)} %reshape.48, f32[80,9216]{1,0:T(8,128)} %tile.9, bf16[80,9216]{1,0:T(8,128)(2,1)} %all-reduce.5.cloned.1.call-done, bf16[80,9216]{1,0:T(8,128)(2,1)} %all-reduce.3.cloned.1.call-done), kind=kLoop, calls=%fused_computation.20 | loop fusion | flops 11796480 | bytes 10321920 | tf_op jit(solution)/shard_map/convert_element_type | solution.py:79
  223.6 1.4 reshape.47
  (9 shorter events, 0.1 us)
Async XLA Ops:
  6.5 34.5 %copy-start = (bf16[1,512,1024]{2,1,0:T(8,128)(2,1)S(1)}, bf16[1,512,1024]{2,1,0:T(8,128)(2,1)}, u32[]{:S(2)}) copy-start(bf16[1,512,1024]{2,1,0:T(8,128)(2,1)} %param.15) | copy-start | bytes 3145732
  6.5 18.5 %copy-start.1 = (bf16[1,20,4,9216]{3,2,1,0:T(4,128)(2,1)S(1)}, bf16[1,20,4,9216]{3,2,1,0:T(4,128)(2,1)}, u32[]{:S(2)}) copy-start(bf16[1,20,4,9216]{3,2,1,0:T(4,128)(2,1)} %param.9) | copy-start | bytes 4423684
  6.5 44.1 %reduce-scatter.3.cloned.1.call-start = ((), (), s32[]{:S(2)}) async-start(), calls=%async_computation.2 | async-start | bytes 122880 | tf_op jit(solution)/shard_map/reduce_scatter | solution.py:58
  7.4 20.3 %copy-start.5 = (s32[4]{0:T(128)S(1)}, s32[4]{0:T(128)}, u32[]{:S(2)}) copy-start(s32[4]{0:T(128)} %param.11) | copy-start | bytes 52
  28.0 2.8 %copy-start.6 = (bf16[4,96,256,1]{2,0,1,3:T(4,128)(2,1)}, bf16[4,96,256,1]{2,0,1,3:T(4,128)(2,1)S(1)}, u32[]{:S(2)}) copy-start(bf16[4,96,256,1]{2,0,1,3:T(4,128)(2,1)S(1)} %fusion.16) | copy-start | bytes 589828
  41.0 2.9 %copy-start.4 = (s32[1,4,2]{1,2,0:T(2,128)S(1)}, s32[1,4,2]{1,2,0:T(2,128)}, u32[]{:S(2)}) copy-start(s32[1,4,2]{1,2,0:T(2,128)} %param.10) | copy-start | bytes 100
  42.1 9.3 %copy-start.7 = (bf16[4,96,256,1]{2,0,1,3:T(4,128)(2,1)S(1)}, bf16[4,96,256,1]{2,0,1,3:T(4,128)(2,1)}, u32[]{:S(2)}) copy-start(bf16[4,96,256,1]{2,0,1,3:T(4,128)(2,1)} %copy-done.6) | copy-start | bytes 589828
  42.1 78.7 %all-reduce.3.cloned.1.call-start = ((), (), s32[]{:S(2)}) async-start(), calls=%async_computation.3 | async-start | bytes 2949120 | tf_op jit(solution)/shard_map/psum | solution.py:82
  57.5 3.7 %copy-start.2 = (f32[4,96]{1,0:T(4,128)S(1)}, f32[4,96]{1,0:T(4,128)}, u32[]{:S(2)}) copy-start(f32[4,96]{1,0:T(4,128)} %param.13) | copy-start | bytes 4612
  57.5 4.2 %copy-start.3 = (f32[4,96]{1,0:T(4,128)S(1)}, f32[4,96]{1,0:T(4,128)}, u32[]{:S(2)}) copy-start(f32[4,96]{1,0:T(4,128)} %param.14) | copy-start | bytes 4612
  61.1 87.5 %reduce-scatter.5.cloned.1.call-start = ((), (), s32[]{:S(2)}) async-start(), calls=%async_computation.4 | async-start | bytes 122880 | tf_op jit(solution)/shard_map/reduce_scatter | solution.py:58
  124.6 2.9 %copy-start.8 = (bf16[4,96,256,1]{2,0,1,3:T(4,128)(2,1)S(1)}, bf16[4,96,256,1]{2,0,1,3:T(4,128)(2,1)}, u32[]{:S(2)}) copy-start(bf16[4,96,256,1]{2,0,1,3:T(4,128)(2,1)} %copy-done.6) | copy-start | bytes 589828
  140.9 77.9 %all-reduce.5.cloned.1.call-start = ((), (), s32[]{:S(2)}) async-start(), calls=%async_computation.5 | async-start | bytes 2949120 | tf_op jit(solution)/shard_map/psum | solution.py:82
Sparse Core Ops, SparseCore 0:
  42.2 8.3 reduce-scatter.2
  61.3 59.5 all-reduce.2
  141.1 7.5 reduce-scatter.4
  159.2 59.5 all-reduce.4
where the time goes:
time: 232 us
  waiting for transfers between devices  125 us (54%)
  blocking collectives  36.2 us (16%)
  local copies, waits for them, and re-layouts  32.7 us (14%)
  matrix products  14.8 us (6%)
  between operations  13.3 us (6%)
  other arithmetic  8.91 us (4%)
    psum x2, waiting for transfers between devices, finish(): lax.psum(partial_term.astype(jnp.bfloat16), ('row', 'col'))  111 us
    all_gather x2, blocking collectives, kernel_term(): everywhere = lax.all_gather(values, ('row', 'col'), axis=1, tiled=True)  19.6 us
    all_gather x1, blocking collectives, fetch_each(): found = pick(lax.all_gather(orbitals, 'pb', axis=0, tiled=True))  16.6 us
    reduce_scatter x2, waiting for transfers between devices, kernel_term(): lax.psum_scatter(partial_value.astype(jnp.bfloat16), 'col', scatter_dimen...  14.1 us
    convert_element_type x4, local copies, waits for them, and re-layouts, finish(): partial_term.astype(jnp.bfloat16)  13.5 us
    another operation x2, local copies, waits for them, and re-layouts, on_device(): gap_rows = jnp.tile(gap_grid, (vectors, 1))  6.56 us
    dot_general x2, matrix products, kernel_term(): jnp.einsum('kyqz,yhz->kyqh', weighted_product, conduction_orbital, prefer...  5.75 us
    dot_general x2, matrix products, kernel_term(): jnp.einsum('iomx,oxj->iomj', amplitude_lattice, conduction_orbital, prefe...  5.54 us
  transfers between devices with their start and end apart: 4, of which 4 were waited for; matrix products, arithmetic and copies ran while one was open for 4% of the time, Pallas kernels for 0%

commit v1 on v0

--- a/solution.py
+++ b/solution.py
@@ -5,6 +5,12 @@
 
 CENTER = 3.0
 HALF = 2.5
+
+
+def place_series_all_over_axis(point):
+    for ix in ("col", "row"):
+        point = lax.psum(point, ix)
+    return point
 
 
 def on_device(amplitudes, pairs, stored_k, orbitals, valence_energy, conduction_energy, screened):
@@ -79,7 +85,7 @@
         return (factor * value - previous_rows).astype(jnp.bfloat16)
 
     def finish(partial_term, current, previous, factor):
-        summed = lax.psum(partial_term.astype(jnp.bfloat16), ("row", "col")).astype(jnp.float32)
+        summed = place_series_all_over_axis(partial_term.astype(jnp.bfloat16)).astype(jnp.float32)
         previous_full = None
         if previous is not None:
             previous_full = previous.astype(jnp.float32)

time: 232 us -> 287 us (1.24)
  waiting for transfers between devices: 125 us -> 176 us
    psum x2 -> x4, waiting for transfers between devices: 111 us -> 160 us  [place_series_all_over_axis(): point = lax.psum(point, ix)]
  transfers between devices with their start and end apart: 4 -> 6, of which waited for: 4 -> 6; matrix products, arithmetic and copies ran while one was open for 4% -> 3% of each run, Pallas kernels for 0% -> 0%
where the time goes in v1:
time: 287 us; the launch traced here: 286 us
  waiting for transfers between devices  176 us (61%)
  blocking collectives  36.8 us (13%)
  local copies, waits for them, and re-layouts  34.9 us (12%)
  matrix products  14.8 us (5%)
  between operations  13.7 us (5%)
  other arithmetic  9.7 us (3%)
    psum x4, waiting for transfers between devices, place_series_all_over_axis(): point = lax.psum(point, ix)  160 us
    all_gather x2, blocking collectives, kernel_term(): everywhere = lax.all_gather(values, ('row', 'col'), axis=1, tiled=True)  20.2 us
    all_gather x1, blocking collectives, fetch_each(): found = pick(lax.all_gather(orbitals, 'pb', axis=0, tiled=True))  16.6 us
    reduce_scatter x2, waiting for transfers between devices, kernel_term(): lax.psum_scatter(partial_value.astype(jnp.bfloat16), 'col', scatter_dimen...  15.9 us
    convert_element_type x4, local copies, waits for them, and re-layouts, finish(): partial_term.astype(jnp.bfloat16)  13.5 us
    another operation x2, local copies, waits for them, and re-layouts, on_device(): gap_rows = jnp.tile(gap_grid, (vectors, 1))  6.53 us
    dot_general x2, matrix products, kernel_term(): jnp.einsum('kyqz,yhz->kyqh', weighted_product, conduction_orbital, prefer...  5.76 us
  transfers between devices with their start and end apart: 6, of which 6 were waited for; matrix products, arithmetic and copies ran while one was open for 3% of the time, Pallas kernels for 0%

profile of v1, /device:TPU:0, one launch (start us, length us, event | category | flops | bytes accessed | tf_op | source)
XLA Modules:
  0.0 286.2 jit_solution(8528285945165947028)
XLA Ops:
  6.5 0.0 copy-start
  6.5 0.0 reduce-scatter.3.cloned.1.call-start
  6.5 0.8 slice_bitcast_fusion.1
  7.4 16.6 %all_gather.10 = bf16[4,192,256]{2,1,0:T(8,128)(2,1)S(1)} all-gather(bf16[1,192,256]{2,1,0:T(8,128)(2,1)} %param.12), channel_id=1, replica_groups=mesh['pb'=4,'row'=4,'col'=2] {'pb'}, dimensions={0}, use_global_device_ids=true | all-gather | bytes 491520 | tf_op jit(solution)/shard_map/all_gather | solution.py:39
  24.0 1.0 fusion.15
  25.0 0.1 copy.59
  25.1 0.0 copy-done.2
  25.1 2.6 reshape_reshape_squeeze.3
  27.7 0.0 copy-done.7
  27.7 0.3 fusion.16
  28.0 0.0 copy-start.8
  28.0 2.8 fusion.1
  30.9 10.1 %all_gather.11 = bf16[80,2048]{1,0:T(8,128)(2,1)S(1)} all-gather(bf16[80,256]{1,0:T(8,128)(2,1)S(1)} %convert_element_type.92), channel_id=1, replica_groups=mesh['pb'=4,'row'=4,'col'=2] {'row','col'}, dimensions={1}, use_global_device_ids=true | all-gather | bytes 368640 | tf_op jit(solution)/shard_map/all_gather | solution.py:58
  41.0 0.0 copy-done
  41.0 1.1 convolution_convert_fusion.3
  42.1 0.0 reduce-scatter.3.cloned.1.call-update
  42.1 0.0 all-reduce.5.cloned.1.call-start
  42.1 8.4 %reduce-scatter.3.cloned.1.call-done = bf16[80,256]{1,0:T(8,128)(2,1)} async-done(((bf16[80,512]{1,0:T(8,128)(2,1)}), bf16[80,256]{1,0:T(8,128)(2,1)}) %reduce-scatter.3.cloned.1.call-update) | async-done | bytes 40976 | tf_op jit(solution)/shard_map/reduce_scatter | solution.py:64
  50.6 0.8 reshape.49
  51.4 0.0 copy-done.8
  51.4 2.9 %convert_bitcast_fusion.1 = bf16[20,4,96,96]{2,3,0,1:T(8,128)(2,1)} fusion(f32[20,4,256]{2,0,1:T(8,128)S(1)} %copy.63, f32[4,96,256]{2,1,0:T(8,128)S(1)} %copy.59, bf16[4,96,256,1]{2,0,1,3:T(4,128)(2,1)S(1)} %fusion.16), kind=kOutput, calls=%fused_computation.25 | convolution fusion | flops 382156800 | bytes 2146304 | tf_op jit(solution)/shard_map/kyqz,yhz->kyqh/dot_general | solution.py:73
  54.3 3.2 %copy.65 = bf16[20,4,96,96]{3,2,1,0:T(8,128)(2,1)S(1)} copy(bf16[20,4,96,96]{2,3,0,1:T(8,128)(2,1)} %convert_bitcast_fusion.1) | data formatting | bytes 2949120 | tf_op jit(solution)/shard_map/convert_element_type | solution.py:88
  57.5 3.6 %convert_element_type.97 = bf16[80,9216]{1,0:T(8,128)(2,1)} reshape(bf16[20,4,96,96]{3,2,1,0:T(8,128)(2,1)S(1)} %copy.65) | data formatting | bytes 2949120 | tf_op jit(solution)/shard_map/convert_element_type | solution.py:88
  61.1 0.0 all-reduce.5.cloned.1.call-update
  61.1 0.0 all-reduce.7.cloned.1.call-start
  61.1 21.4 %all-reduce.5.cloned.1.call-done = bf16[80,9216]{1,0:T(8,128)(2,1)} async-done(((bf16[80,9216]{1,0:T(8,128)(2,1)}), bf16[80,9216]{1,0:T(8,128)(2,1)}) %all-reduce.5.cloned.1.call-update) | async-done | bytes 1474576 | tf_op jit(solution)/shard_map/psum | solution.py:12
  82.6 0.0 all-reduce.7.cloned.1.call-update
  82.6 0.0 reduce-scatter.5.cloned.1.call-start
  82.6 0.0 copy-done.3
  82.7 1.7 reshape.48
  84.4 0.0 copy-done.6
  84.4 0.0 copy-done.4
  84.4 0.6 gather_fusion.1
  85.0 0.0 copy-done.5
  85.0 0.6 gather_fusion
  85.5 0.1 broadcast_select_fusion
  85.6 0.1 broadcast_select_fusion.1
  85.7 0.1 broadcast_subtract_fusion
  85.8 0.2 sub.32
  86.0 2.3 tile.8
  88.3 4.3 %tile.9 = f32[80,9216]{1,0:T(8,128)} reshape(f32[20,4,9216]{2,1,0:T(4,128)} %tile.8) | data formatting | bytes 5898240 | tf_op jit(solution)/shard_map/tile | solution.py:45
  92.5 53.7 %all-reduce.7.cloned.1.call-done = bf16[80,9216]{1,0:T(8,128)(2,1)} async-done(((bf16[80,9216]{1,0:T(8,128)(2,1)}), bf16[80,9216]{1,0:T(8,128)(2,1)}) %all-reduce.7.cloned.1.call-update) | async-done | bytes 1474576 | tf_op jit(solution)/shard_map/psum | solution.py:12
  146.2 3.8 %multiply_convert_fusion.4 = bf16[80,9216]{1,0:T(8,128)(2,1)S(1)} fusion(f32[80,9216]{1,0:T(8,128)} %reshape.48, bf16[80,9216]{1,0:T(8,128)(2,1)} %all-reduce.7.cloned.1.call-done, f32[80,9216]{1,0:T(8,128)} %tile.9), kind=kLoop, calls=%fused_computation.21 | loop fusion | flops 5160960 | bytes 8847360 | tf_op jit(solution)/shard_map/convert_element_type | solution.py:84
  150.0 0.0 copy-start.9
  150.0 2.9 %reshape.46 = bf16[20,4,96,96]{3,2,1,0:T(8,128)(2,1)} reshape(bf16[80,9216]{1,0:T(8,128)(2,1)S(1)} %multiply_convert_fusion.4) | data formatting | bytes 2949120 | tf_op jit(solution)/shard_map/reshape | solution.py:49
  152.9 0.0 copy-done.9
  152.9 2.7 fusion
  155.7 10.1 %all_gather.12 = bf16[80,2048]{1,0:T(8,128)(2,1)S(1)} all-gather(bf16[80,256]{1,0:T(8,128)(2,1)S(1)} %convert_element_type.102), channel_id=1, replica_groups=mesh['pb'=4,'row'=4,'col'=2] {'row','col'}, dimensions={1}, use_global_device_ids=true | all-gather | bytes 368640 | tf_op jit(solution)/shard_map/all_gather | solution.py:58
  165.8 1.1 convolution_convert_fusion.2
  166.9 0.0 reduce-scatter.5.cloned.1.call-update
  166.9 0.2 all-reduce.9.cloned.1.call-start
  167.1 7.5 %reduce-scatter.5.cloned.1.call-done = bf16[80,256]{1,0:T(8,128)(2,1)} async-done(((bf16[80,512]{1,0:T(8,128)(2,1)}), bf16[80,256]{1,0:T(8,128)(2,1)}) %reduce-scatter.5.cloned.1.call-update) | async-done | bytes 40976 | tf_op jit(solution)/shard_map/reduce_scatter | solution.py:64
  174.6 0.8 reshape.50
  175.4 2.9 convert_bitcast_fusion
  178.3 3.2 %copy.71 = bf16[20,4,96,96]{3,2,1,0:T(8,128)(2,1)S(1)} copy(bf16[20,4,96,96]{2,3,0,1:T(8,128)(2,1)} %convert_bitcast_fusion) | data formatting | bytes 2949120 | tf_op jit(solution)/shard_map/convert_element_type | solution.py:88
  181.5 3.6 %convert_element_type.107 = bf16[80,9216]{1,0:T(8,128)(2,1)} reshape(bf16[20,4,96,96]{3,2,1,0:T(8,128)(2,1)S(1)} %copy.71) | data formatting | bytes 2949120 | tf_op jit(solution)/shard_map/convert_element_type | solution.py:88
  185.1 0.0 all-reduce.9.cloned.1.call-update
  185.1 0.0 all-reduce.11.cloned.1.call-start
  185.1 21.4 %all-reduce.9.cloned.1.call-done = bf16[80,9216]{1,0:T(8,128)(2,1)} async-done(((bf16[80,9216]{1,0:T(8,128)(2,1)}), bf16[80,9216]{1,0:T(8,128)(2,1)}) %all-reduce.9.cloned.1.call-update) | async-done | bytes 1474576 | tf_op jit(solution)/shard_map/psum | solution.py:12
  206.6 0.0 all-reduce.11.cloned.1.call-update
  206.6 63.5 %all-reduce.11.cloned.1.call-done = bf16[80,9216]{1,0:T(8,128)(2,1)} async-done(((bf16[80,9216]{1,0:T(8,128)(2,1)}), bf16[80,9216]{1,0:T(8,128)(2,1)}) %all-reduce.11.cloned.1.call-update) | async-done | bytes 1474576 | tf_op jit(solution)/shard_map/psum | solution.py:12
  270.0 0.0 copy-done.1
  270.0 5.6 %fusion.12 = bf16[80,9216]{1,0:T(8,128)(2,1)} fusion(f32[80,9216]{1,0:T(8,128)} %reshape.48, f32[80,9216]{1,0:T(8,128)} %tile.9, bf16[80,9216]{1,0:T(8,128)(2,1)} %all-reduce.11.cloned.1.call-done, bf16[80,9216]{1,0:T(8,128)(2,1)S(1)} %copy-done.1), kind=kLoop, calls=%fused_computation.20 | loop fusion | flops 11796480 | bytes 10321920 | tf_op jit(solution)/shard_map/convert_element_type | solution.py:85
  275.7 3.6 %reshape.47 = bf16[1,20,4,9216]{3,2,1,0:T(4,128)(2,1)} reshape(bf16[80,9216]{1,0:T(8,128)(2,1)} %fusion.12) | data formatting | bytes 2949120 | tf_op jit(solution)/shard_map/reshape | solution.py:99
  (16 shorter events, 0.2 us)
Async XLA Ops:
  6.5 34.4 %copy-start = (bf16[1,512,1024]{2,1,0:T(8,128)(2,1)S(1)}, bf16[1,512,1024]{2,1,0:T(8,128)(2,1)}, u32[]{:S(2)}) copy-start(bf16[1,512,1024]{2,1,0:T(8,128)(2,1)} %param.15) | copy-start | bytes 3145732
  6.5 18.5 %copy-start.2 = (bf16[1,20,4,9216]{3,2,1,0:T(4,128)(2,1)S(1)}, bf16[1,20,4,9216]{3,2,1,0:T(4,128)(2,1)}, u32[]{:S(2)}) copy-start(bf16[1,20,4,9216]{3,2,1,0:T(4,128)(2,1)} %param.9) | copy-start | bytes 4423684
  6.5 44.0 %reduce-scatter.3.cloned.1.call-start = ((), (), s32[]{:S(2)}) async-start(), calls=%async_computation.2 | async-start | bytes 122880 | tf_op jit(solution)/shard_map/reduce_scatter | solution.py:64
  7.4 20.3 %copy-start.7 = (s32[4]{0:T(128)S(1)}, s32[4]{0:T(128)}, u32[]{:S(2)}) copy-start(s32[4]{0:T(128)} %param.11) | copy-start | bytes 52
  28.0 23.4 %copy-start.8 = (bf16[4,96,256,1]{2,0,1,3:T(4,128)(2,1)}, bf16[4,96,256,1]{2,0,1,3:T(4,128)(2,1)S(1)}, u32[]{:S(2)}) copy-start(bf16[4,96,256,1]{2,0,1,3:T(4,128)(2,1)S(1)} %fusion.16) | copy-start | bytes 589828
  42.1 40.5 %all-reduce.5.cloned.1.call-start = ((), (), s32[]{:S(2)}) async-start(), calls=%async_computation.3 | async-start | bytes 2949120 | tf_op jit(solution)/shard_map/psum | solution.py:12
  61.1 21.6 %copy-start.3 = (bf16[1,20,4,9216]{3,2,1,0:T(4,128)(2,1)S(1)}, bf16[1,20,4,9216]{3,2,1,0:T(4,128)(2,1)}, u32[]{:S(2)}) copy-start(bf16[1,20,4,9216]{3,2,1,0:T(4,128)(2,1)} %param.9) | copy-start | bytes 4423684
  61.1 85.1 %all-reduce.7.cloned.1.call-start = ((), (), s32[]{:S(2)}) async-start(), calls=%async_computation.4 | async-start | bytes 2949120 | tf_op jit(solution)/shard_map/psum | solution.py:12
  82.6 1.8 copy-start.6
  82.6 1.8 copy-start.4
  82.6 2.4 copy-start.5
  82.6 92.0 %reduce-scatter.5.cloned.1.call-start = ((), (), s32[]{:S(2)}) async-start(), calls=%async_computation.5 | async-start | bytes 122880 | tf_op jit(solution)/shard_map/reduce_scatter | solution.py:64
  150.0 2.9 %copy-start.9 = (bf16[4,96,256,1]{2,0,1,3:T(4,128)(2,1)S(1)}, bf16[4,96,256,1]{2,0,1,3:T(4,128)(2,1)}, u32[]{:S(2)}) copy-start(bf16[4,96,256,1]{2,0,1,3:T(4,128)(2,1)} %copy-done.8) | copy-start | bytes 589828
  166.9 39.6 %all-reduce.9.cloned.1.call-start = ((), (), s32[]{:S(2)}) async-start(), calls=%async_computation.6 | async-start | bytes 2949120 | tf_op jit(solution)/shard_map/psum | solution.py:12
  185.1 85.0 %copy-start.1 = (bf16[80,9216]{1,0:T(8,128)(2,1)S(1)}, bf16[80,9216]{1,0:T(8,128)(2,1)}, u32[]{:S(2)}) copy-start(bf16[80,9216]{1,0:T(8,128)(2,1)} %all-reduce.7.cloned.1.call-done) | copy-start | bytes 4423684
  185.1 85.0 %all-reduce.11.cloned.1.call-start = ((), (), s32[]{:S(2)}) async-start(), calls=%async_computation.7 | async-start | bytes 2949120 | tf_op jit(solution)/shard_map/psum | solution.py:12
Sparse Core Ops, SparseCore 0:
  42.2 8.3 reduce-scatter.2
  61.2 21.3 all-reduce.4
  85.7 60.4 all-reduce.6
  167.0 7.5 reduce-scatter.4
  185.2 21.3 all-reduce.8
  209.6 60.4 all-reduce.10
